TPU v7x, 32 devices: a whole 2x2x4 slice. The times are simulated.
32 devices in a mesh: group: 4 (over y, core), shard: 8 (over z, x).
Axes of the slice: x: 2, y: 2, z: 4, core: 2. Of those that a mesh axis runs over, the one named last changes fastest.
Arguments:
- queries: bfloat16 [512, 32, 128], P(('group', 'shard')), may hold values from -12 to 12
- passages: bfloat16 [2048, 64, 128], P(('group', 'shard')), may hold values from -4 to 4
- candidates: int32 [512, 160], P(('group', 'shard')), may hold values from 0 to 2047, as said below
- passage_slot: int32 [2048], replicated, may hold values from 0 to 2047, as said below
Outputs:
- scores: float32 [512, 160], P(('group', 'shard'))
Inputs may be any that keep to these rules, and one draw needn't show every extreme that they name: `passage_slot`: every storage row is named by exactly one passage id. `candidates`: candidates k * 20 to (k + 1) * 20 - 1 of a query, for k < 8, all lie in the storage rows of one device, rows d * 64 to (d + 1) * 64 - 1 of device d counted group-major. Over the 16 queries of one device, at most 12 such groups name any one device, and some devices are named exactly 12 times by the queries of every device.
All inputs are finite; a program needn't handle non-finite values.
Results may differ from a plain program's by a relative error of at most 0.0003.
Values may be sent and summed in bfloat16 or wider, within the bound.
No kernel may reach another device: no remote copies, remote signals or barrier semaphores. Data moves between devices by JAX's collectives and lax.ppermute only.
A program may use at most 64 MiB of HBM per device.

v0:
```python
import jax
import jax.numpy as jnp
from jax import lax
from jax.sharding import PartitionSpec as P

PER_VISIT = 20


def score_visits(query_rows, local_rows, passages):
    item_count, peer_width, qtok_count, dim_count = query_rows.shape
    slot_count, ptok_count = (passages.shape[0], passages.shape[1])
    visit_total = item_count * peer_width
    block_size = 16
    store_flat = passages.reshape(slot_count * ptok_count, dim_count)
    query_blocks = query_rows.reshape(visit_total // block_size, block_size, qtok_count, dim_count)
    row_blocks = local_rows.reshape(visit_total // block_size, block_size, local_rows.shape[2])
    slot_ids = jnp.arange(slot_count, dtype=jnp.int32)

    def one_block(pieces):
        query_block, row_block = pieces
        similarity = jnp.einsum(
            "vqd,sd->vqs", query_block, store_flat, preferred_element_type=jnp.float32
        )
        best_match = jnp.max(
            similarity.reshape(block_size, qtok_count, slot_count, ptok_count), axis=3
        )
        passage_score = jnp.sum(best_match, axis=1) / qtok_count
        picker = (row_block[:, :, None] == slot_ids[None, None, :]).astype(jnp.float32)
        return jnp.sum(picker * passage_score[:, None, :], axis=2)

    visit_scores = lax.map(one_block, (query_blocks, row_blocks))
    visit_scores = visit_scores.reshape(item_count, peer_width, local_rows.shape[2])
    return lax.all_to_all(visit_scores, ("group", "shard"), split_axis=1, concat_axis=1, tiled=True)


def local(queries, passages, candidates, passage_slot):
    peer_count = lax.axis_size(("group", "shard"))
    query_count, cand_count = candidates.shape
    slot_count = passages.shape[0]
    spread_count = cand_count // PER_VISIT
    capacity = 3 * query_count * spread_count // peer_count
    visit_count = query_count * spread_count
    storage = passage_slot[candidates].reshape(visit_count, PER_VISIT)
    target = storage[:, 0] // slot_count
    local_rows = storage % slot_count
    matches = (target[:, None] == jnp.arange(peer_count, dtype=jnp.int32)[None, :]).astype(
        jnp.int32
    )
    before = jnp.cumsum(matches, axis=0) - matches
    rank_in = jnp.sum(before * matches, axis=1)
    position = rank_in * peer_count + target
    holder = (
        jnp.zeros((capacity * peer_count,), jnp.int32)
        .at[position]
        .set(jnp.arange(visit_count, dtype=jnp.int32))
    )
    send_local = local_rows[holder].reshape(capacity, peer_count, PER_VISIT)
    query_local = holder // spread_count
    everyone = lax.all_gather(queries, ("group", "shard"), axis=0, tiled=True)
    query_global = (lax.axis_index(("group", "shard")) * query_count + query_local).reshape(
        capacity, peer_count
    )
    wanted = lax.all_to_all(
        query_global, ("group", "shard"), split_axis=1, concat_axis=1, tiled=True
    )
    local_block = lax.all_to_all(
        send_local, ("group", "shard"), split_axis=1, concat_axis=1, tiled=True
    )
    returned = score_visits(everyone[wanted], local_block, passages)
    flat_scores = returned.reshape(capacity * peer_count, PER_VISIT)[position]
    return flat_scores.reshape(query_count, cand_count)


def solution(mesh):
    return jax.shard_map(
        local,
        mesh=mesh,
        in_specs=(
            P(("group", "shard"), None, None),
            P(("group", "shard"), None, None),
            P(("group", "shard"), None),
            P(),
        ),
        out_specs=P(("group", "shard"), None),
        check_vma=False,
    )
```

profile of v0, /device:TPU:0, one launch (start us, length us, event | category | flops | bytes accessed | tf_op | source)
XLA Modules:
  0.0 248.6 jit_solution(6655536599872342939)
XLA Ops:
  8.1 13.6 %gather_fusion = s32[2560]{0:T(1024)S(1)} fusion(s32[2048]{0:T(1024)S(1)} %copy-done, s32[3072]{0:T(1024)S(1)} %pad_clamp_fusion), kind=kCustom, calls=%fused_computation | custom fusion | bytes 30720 | tf_op jit(solution)/shard_map/gather | solution.py:43
  24.4 7.3 %all-to-all-start.1 = ((s32[12,32,1]{0,2,1:T(1,128)}), s32[12,32,1]{0,2,1:T(1,128)S(1)}, u32[]{:S(2)}, u32[]{:S(2)}) async-start(s32[12,32,1]{0,2,1:T(1,128)} %copy.19), calls=%async_computation.1 | async-start | bytes 32768 | tf_op jit(solution)/shard_map/all_to_all | solution.py:63
  41.6 7.0 %all-to-all-done = s32[32,1,240]{2,1,0:T(1,128)S(1)} async-done(((s32[32,1,240]{2,1,0:T(1,128)}), s32[32,1,240]{2,1,0:T(1,128)S(1)}, u32[]{:S(2)}, u32[]{:S(2)}) %all-to-all-start) | async-done | bytes 30752 | tf_op jit(solution)/shard_map/all_to_all | solution.py:66
  50.1 24.7 %all-gather.2.cloned.1.call-done = bf16[512,32,128]{2,1,0:T(8,128)(2,1)} async-done(((bf16[16,32,128]{2,1,0:T(8,128)(2,1)}), bf16[512,32,128]{2,1,0:T(8,128)(2,1)}) %all-gather.2.cloned.1.call-update) | async-done | bytes 4194320 | tf_op jit(solution)/shard_map/all_gather | solution.py:59
  79.7 147.7 %while.11 = (s32[]{:T(128)}, f32[24,16,20]{2,1,0:T(8,128)S(1)}, s32[24,16,20]{2,1,0:T(8,128)S(1)}, bf16[24,16,32,128]{3,2,1,0:T(8,128)(2,1)}, bf16[4096,128]{1,0:T(8,128)(2,1)S(1)}, /*index=5*/s32[]{:T(128)}, f32[]{:T(128)}) while((s32[]{:T(128)}, f32[24,16,20]{2,1,0:T(8,128)S(1)}, s32[24,16,20]{2,1,0:T(8,128)S(1)}, ...), condition=%wide.region_7.8_spmd.clone, body=%wide.region_3.7_spmd.clone.sunk | while | flops 539029184 | bytes 1484901 | solution.py:31
  79.8 5.5 %convolution_reduce_fusion.2 = f32[16,32,64]{1,2,0:T(8,128)S(1)} fusion(bf16[64,64,128,1]{2,1,0,3:T(8,128)(2,1)S(1)} %bitcast.53, bf16[24,16,32,128]{3,2,1,0:T(8,128)(2,1)} %get-tuple-element.110, s32[]{:T(128)S(6)} %copy.35), kind=kOutput, calls=%fused_computation.6.clone.1 | convolution fusion | flops 538935296 | bytes 1310724 | tf_op jit(solution)/shard_map/while/body/eval_jaxpr/vqd,sd->vqs/dot_general | solution.py:21
  92.1 5.5 %convolution_reduce_fusion.2 = f32[16,32,64]{1,2,0:T(8,128)S(1)} fusion(bf16[64,64,128,1]{2,1,0,3:T(8,128)(2,1)S(1)} %bitcast.53, bf16[24,16,32,128]{3,2,1,0:T(8,128)(2,1)} %get-tuple-element.110, s32[]{:T(128)S(6)} %copy.35), kind=kOutput, calls=%fused_computation.6.clone.1 | convolution fusion | flops 538935296 | bytes 1310724 | tf_op jit(solution)/shard_map/while/body/eval_jaxpr/vqd,sd->vqs/dot_general | solution.py:21
  98.3 5.5 %convolution_reduce_fusion.2 = f32[16,32,64]{1,2,0:T(8,128)S(1)} fusion(bf16[64,64,128,1]{2,1,0,3:T(8,128)(2,1)S(1)} %bitcast.53, bf16[24,16,32,128]{3,2,1,0:T(8,128)(2,1)} %get-tuple-element.110, s32[]{:T(128)S(6)} %copy.35), kind=kOutput, calls=%fused_computation.6.clone.1 | convolution fusion | flops 538935296 | bytes 1310724 | tf_op jit(solution)/shard_map/while/body/eval_jaxpr/vqd,sd->vqs/dot_general | solution.py:21
  104.5 5.5 %convolution_reduce_fusion.2 = f32[16,32,64]{1,2,0:T(8,128)S(1)} fusion(bf16[64,64,128,1]{2,1,0,3:T(8,128)(2,1)S(1)} %bitcast.53, bf16[24,16,32,128]{3,2,1,0:T(8,128)(2,1)} %get-tuple-element.110, s32[]{:T(128)S(6)} %copy.35), kind=kOutput, calls=%fused_computation.6.clone.1 | convolution fusion | flops 538935296 | bytes 1310724 | tf_op jit(solution)/shard_map/while/body/eval_jaxpr/vqd,sd->vqs/dot_general | solution.py:21
  116.8 5.5 %convolution_reduce_fusion.2 = f32[16,32,64]{1,2,0:T(8,128)S(1)} fusion(bf16[64,64,128,1]{2,1,0,3:T(8,128)(2,1)S(1)} %bitcast.53, bf16[24,16,32,128]{3,2,1,0:T(8,128)(2,1)} %get-tuple-element.110, s32[]{:T(128)S(6)} %copy.35), kind=kOutput, calls=%fused_computation.6.clone.1 | convolution fusion | flops 538935296 | bytes 1310724 | tf_op jit(solution)/shard_map/while/body/eval_jaxpr/vqd,sd->vqs/dot_general | solution.py:21
  122.9 5.5 %convolution_reduce_fusion.2 = f32[16,32,64]{1,2,0:T(8,128)S(1)} fusion(bf16[64,64,128,1]{2,1,0,3:T(8,128)(2,1)S(1)} %bitcast.53, bf16[24,16,32,128]{3,2,1,0:T(8,128)(2,1)} %get-tuple-element.110, s32[]{:T(128)S(6)} %copy.35), kind=kOutput, calls=%fused_computation.6.clone.1 | convolution fusion | flops 538935296 | bytes 1310724 | tf_op jit(solution)/shard_map/while/body/eval_jaxpr/vqd,sd->vqs/dot_general | solution.py:21
  129.1 5.5 %convolution_reduce_fusion.2 = f32[16,32,64]{1,2,0:T(8,128)S(1)} fusion(bf16[64,64,128,1]{2,1,0,3:T(8,128)(2,1)S(1)} %bitcast.53, bf16[24,16,32,128]{3,2,1,0:T(8,128)(2,1)} %get-tuple-element.110, s32[]{:T(128)S(6)} %copy.35), kind=kOutput, calls=%fused_computation.6.clone.1 | convolution fusion | flops 538935296 | bytes 1310724 | tf_op jit(solution)/shard_map/while/body/eval_jaxpr/vqd,sd->vqs/dot_general | solution.py:21
  141.4 5.5 %convolution_reduce_fusion.2 = f32[16,32,64]{1,2,0:T(8,128)S(1)} fusion(bf16[64,64,128,1]{2,1,0,3:T(8,128)(2,1)S(1)} %bitcast.53, bf16[24,16,32,128]{3,2,1,0:T(8,128)(2,1)} %get-tuple-element.110, s32[]{:T(128)S(6)} %copy.35), kind=kOutput, calls=%fused_computation.6.clone.1 | convolution fusion | flops 538935296 | bytes 1310724 | tf_op jit(solution)/shard_map/while/body/eval_jaxpr/vqd,sd->vqs/dot_general | solution.py:21
  147.5 5.5 %convolution_reduce_fusion.2 = f32[16,32,64]{1,2,0:T(8,128)S(1)} fusion(bf16[64,64,128,1]{2,1,0,3:T(8,128)(2,1)S(1)} %bitcast.53, bf16[24,16,32,128]{3,2,1,0:T(8,128)(2,1)} %get-tuple-element.110, s32[]{:T(128)S(6)} %copy.35), kind=kOutput, calls=%fused_computation.6.clone.1 | convolution fusion | flops 538935296 | bytes 1310724 | tf_op jit(solution)/shard_map/while/body/eval_jaxpr/vqd,sd->vqs/dot_general | solution.py:21
  153.7 5.5 %convolution_reduce_fusion.2 = f32[16,32,64]{1,2,0:T(8,128)S(1)} fusion(bf16[64,64,128,1]{2,1,0,3:T(8,128)(2,1)S(1)} %bitcast.53, bf16[24,16,32,128]{3,2,1,0:T(8,128)(2,1)} %get-tuple-element.110, s32[]{:T(128)S(6)} %copy.35), kind=kOutput, calls=%fused_computation.6.clone.1 | convolution fusion | flops 538935296 | bytes 1310724 | tf_op jit(solution)/shard_map/while/body/eval_jaxpr/vqd,sd->vqs/dot_general | solution.py:21
  166.0 5.5 %convolution_reduce_fusion.2 = f32[16,32,64]{1,2,0:T(8,128)S(1)} fusion(bf16[64,64,128,1]{2,1,0,3:T(8,128)(2,1)S(1)} %bitcast.53, bf16[24,16,32,128]{3,2,1,0:T(8,128)(2,1)} %get-tuple-element.110, s32[]{:T(128)S(6)} %copy.35), kind=kOutput, calls=%fused_computation.6.clone.1 | convolution fusion | flops 538935296 | bytes 1310724 | tf_op jit(solution)/shard_map/while/body/eval_jaxpr/vqd,sd->vqs/dot_general | solution.py:21
  172.2 5.5 %convolution_reduce_fusion.2 = f32[16,32,64]{1,2,0:T(8,128)S(1)} fusion(bf16[64,64,128,1]{2,1,0,3:T(8,128)(2,1)S(1)} %bitcast.53, bf16[24,16,32,128]{3,2,1,0:T(8,128)(2,1)} %get-tuple-element.110, s32[]{:T(128)S(6)} %copy.35), kind=kOutput, calls=%fused_computation.6.clone.1 | convolution fusion | flops 538935296 | bytes 1310724 | tf_op jit(solution)/shard_map/while/body/eval_jaxpr/vqd,sd->vqs/dot_general | solution.py:21
  178.3 5.5 %convolution_reduce_fusion.2 = f32[16,32,64]{1,2,0:T(8,128)S(1)} fusion(bf16[64,64,128,1]{2,1,0,3:T(8,128)(2,1)S(1)} %bitcast.53, bf16[24,16,32,128]{3,2,1,0:T(8,128)(2,1)} %get-tuple-element.110, s32[]{:T(128)S(6)} %copy.35), kind=kOutput, calls=%fused_computation.6.clone.1 | convolution fusion | flops 538935296 | bytes 1310724 | tf_op jit(solution)/shard_map/while/body/eval_jaxpr/vqd,sd->vqs/dot_general | solution.py:21
  190.6 5.5 %convolution_reduce_fusion.2 = f32[16,32,64]{1,2,0:T(8,128)S(1)} fusion(bf16[64,64,128,1]{2,1,0,3:T(8,128)(2,1)S(1)} %bitcast.53, bf16[24,16,32,128]{3,2,1,0:T(8,128)(2,1)} %get-tuple-element.110, s32[]{:T(128)S(6)} %copy.35), kind=kOutput, calls=%fused_computation.6.clone.1 | convolution fusion | flops 538935296 | bytes 1310724 | tf_op jit(solution)/shard_map/while/body/eval_jaxpr/vqd,sd->vqs/dot_general | solution.py:21
  196.8 5.5 %convolution_reduce_fusion.2 = f32[16,32,64]{1,2,0:T(8,128)S(1)} fusion(bf16[64,64,128,1]{2,1,0,3:T(8,128)(2,1)S(1)} %bitcast.53, bf16[24,16,32,128]{3,2,1,0:T(8,128)(2,1)} %get-tuple-element.110, s32[]{:T(128)S(6)} %copy.35), kind=kOutput, calls=%fused_computation.6.clone.1 | convolution fusion | flops 538935296 | bytes 1310724 | tf_op jit(solution)/shard_map/while/body/eval_jaxpr/vqd,sd->vqs/dot_general | solution.py:21
  202.9 5.5 %convolution_reduce_fusion.2 = f32[16,32,64]{1,2,0:T(8,128)S(1)} fusion(bf16[64,64,128,1]{2,1,0,3:T(8,128)(2,1)S(1)} %bitcast.53, bf16[24,16,32,128]{3,2,1,0:T(8,128)(2,1)} %get-tuple-element.110, s32[]{:T(128)S(6)} %copy.35), kind=kOutput, calls=%fused_computation.6.clone.1 | convolution fusion | flops 538935296 | bytes 1310724 | tf_op jit(solution)/shard_map/while/body/eval_jaxpr/vqd,sd->vqs/dot_general | solution.py:21
  215.3 5.5 %convolution_reduce_fusion.2 = f32[16,32,64]{1,2,0:T(8,128)S(1)} fusion(bf16[64,64,128,1]{2,1,0,3:T(8,128)(2,1)S(1)} %bitcast.53, bf16[24,16,32,128]{3,2,1,0:T(8,128)(2,1)} %get-tuple-element.110, s32[]{:T(128)S(6)} %copy.35), kind=kOutput, calls=%fused_computation.6.clone.1 | convolution fusion | flops 538935296 | bytes 1310724 | tf_op jit(solution)/shard_map/while/body/eval_jaxpr/vqd,sd->vqs/dot_general | solution.py:21
  221.4 5.5 %convolution_reduce_fusion.2 = f32[16,32,64]{1,2,0:T(8,128)S(1)} fusion(bf16[64,64,128,1]{2,1,0,3:T(8,128)(2,1)S(1)} %bitcast.53, bf16[24,16,32,128]{3,2,1,0:T(8,128)(2,1)} %get-tuple-element.110, s32[]{:T(128)S(6)} %copy.35), kind=kOutput, calls=%fused_computation.6.clone.1 | convolution fusion | flops 538935296 | bytes 1310724 | tf_op jit(solution)/shard_map/while/body/eval_jaxpr/vqd,sd->vqs/dot_general | solution.py:21
  231.8 7.2 %all-to-all-done.2 = f32[32,1,240]{2,1,0:T(1,128)S(1)} async-done(((f32[32,1,240]{2,1,0:T(1,128)}), f32[32,1,240]{2,1,0:T(1,128)S(1)}, u32[]{:S(2)}, u32[]{:S(2)}) %all-to-all-start.2) | async-done | bytes 30752 | tf_op jit(solution)/shard_map/all_to_all | solution.py:33
  (223 shorter events, 74.7 us)
Async XLA Ops:
  6.5 1.5 copy-start
  6.5 68.3 %all-gather.2.cloned.1.call-start = ((), (), s32[]{:S(2)}) async-start(), calls=%async_computation.3 | async-start | bytes 4325376 | tf_op jit(solution)/shard_map/all_gather | solution.py:59
  24.4 14.4 %all-to-all-start.1 = ((s32[12,32,1]{0,2,1:T(1,128)}), s32[12,32,1]{0,2,1:T(1,128)S(1)}, u32[]{:S(2)}, u32[]{:S(2)}) async-start(s32[12,32,1]{0,2,1:T(1,128)} %copy.19), calls=%async_computation.1 | async-start | bytes 32768 | tf_op jit(solution)/shard_map/all_to_all | solution.py:63
  38.8 9.8 %all-to-all-start = ((s32[32,1,240]{2,1,0:T(1,128)}), s32[32,1,240]{2,1,0:T(1,128)S(1)}, u32[]{:S(2)}, u32[]{:S(2)}) async-start(s32[32,1,240]{2,1,0:T(1,128)} %reshape.105), calls=%async_computation | async-start | bytes 65536 | tf_op jit(solution)/shard_map/all_to_all | solution.py:66
  50.1 29.7 %copy-start.1 = (bf16[64,64,128]{2,1,0:T(8,128)(2,1)S(1)}, bf16[64,64,128]{2,1,0:T(8,128)(2,1)}, u32[]{:S(2)}) copy-start(bf16[64,64,128]{2,1,0:T(8,128)(2,1)} %param.7) | copy-start | bytes 3145732
  228.4 10.6 %all-to-all-start.2 = ((f32[32,1,240]{2,1,0:T(1,128)}), f32[32,1,240]{2,1,0:T(1,128)S(1)}, u32[]{:S(2)}, u32[]{:S(2)}) async-start(f32[32,1,240]{2,1,0:T(1,128)} %reshape.107), calls=%async_computation.2 | async-start | bytes 65536 | tf_op jit(solution)/shard_map/all_to_all | solution.py:33
Sparse Core Ops, SparseCore 0:
  10.3 64.4 all-gather.1
where the time goes:
time: 249 us
  matrix products  133 us (53%)
  waiting for transfers between devices  44.6 us (18%)
  local copies, waits for them, and re-layouts  30.6 us (12%)
  between operations  13.6 us (5%)
  starting transfers between devices  13.3 us (5%)
  other arithmetic  12.9 us (5%)
    dot_general x24, matrix products, one_block(): jnp.einsum('vqd,sd->vqs', query_block, store_flat, preferred_element_type...  133 us
    all_gather x1, waiting for transfers between devices, local(): everyone = lax.all_gather(queries, ('group', 'shard'), axis=0, tiled=True)  24.7 us
    gather x1, local copies, waits for them, and re-layouts, local(): storage = passage_slot[candidates].reshape(visit_count, PER_VISIT)  13.6 us
    all_to_all x1, starting transfers between devices, local(): lax.all_to_all(query_global, ('group', 'shard'), split_axis=1, concat_axi...  7.33 us
    all_to_all x1, waiting for transfers between devices, score_visits(): lax.all_to_all(visit_scores, ('group', 'shard'), split_axis=1, concat_axi...  7.18 us
    all_to_all x1, waiting for transfers between devices, local(): lax.all_to_all(send_local, ('group', 'shard'), split_axis=1, concat_axis=...  7.04 us
    reduce_sum x24, other arithmetic, one_block(): passage_score = jnp.sum(best_match, axis=1) / qtok_count  5.03 us
    all_to_all x1, waiting for transfers between devices, local(): lax.all_to_all(query_global, ('group', 'shard'), split_axis=1, concat_axi...  4.98 us
  transfers between devices with their start and end apart: 4, of which 4 were waited for; matrix products, arithmetic and copies ran while one was open for 8% of the time, Pallas kernels for 0%

commit v1 on v0

--- a/solution.py
+++ b/solution.py
@@ -56,7 +56,14 @@
     )
     send_local = local_rows[holder].reshape(capacity, peer_count, PER_VISIT)
     query_local = holder // spread_count
-    everyone = lax.all_gather(queries, ("group", "shard"), axis=0, tiled=True)
+    ways, here = (lax.axis_size(("group", "shard")), lax.axis_index(("group", "shard")))
+    everyone, reach = (queries, 1)
+    while reach < ways:
+        theirs = lax.ppermute(everyone, ("group", "shard"), [(d, d ^ reach) for d in range(ways)])
+        mine_first = jnp.concatenate([everyone, theirs], axis=0)
+        theirs_first = jnp.concatenate([theirs, everyone], axis=0)
+        everyone = jnp.where(here & reach == 0, mine_first, theirs_first)
+        reach = 2 * reach
     query_global = (lax.axis_index(("group", "shard")) * query_count + query_local).reshape(
         capacity, peer_count
     )

time: 249 us -> 278 us (1.12)
  waiting for transfers between devices: 44.6 us -> 71.5 us
  between operations: 13.6 us -> 0.25 us
  starting transfers between devices: 13.3 us -> 21.6 us
  other arithmetic: 12.9 us -> 19.5 us
    ppermute x0 -> x5, waiting for transfers between devices: none -> 33.9 us  [local(): lax.ppermute(everyone, ('group', 'shard'), [(d, d ^ reach) for d in range...]
    all_gather x1 -> x0, waiting for transfers between devices: 24.7 us -> none  [local(): everyone = lax.all_gather(queries, ('group', 'shard'), axis=0, tiled=True)]
    all_to_all x1, waiting for transfers between devices: 4.98 us -> 23.4 us  [local(): lax.all_to_all(query_global, ('group', 'shard'), split_axis=1, concat_axi...]
    ppermute x0 -> x5, starting transfers between devices: none -> 8.84 us  [local(): lax.ppermute(everyone, ('group', 'shard'), [(d, d ^ reach) for d in range...]
    select_n x0 -> x5, other arithmetic: none -> 7.34 us  [local(): everyone = jnp.where(here & reach == 0, mine_first, theirs_first)]
    all_to_all x1, starting transfers between devices: 2.55 us -> 5.43 us  [local(): lax.all_to_all(send_local, ('group', 'shard'), split_axis=1, concat_axis=...]
  transfers between devices with their start and end apart: 4 -> 8, of which waited for: 4 -> 7; matrix products, arithmetic and copies ran while one was open for 8% -> 7% of each run, Pallas kernels for 0% -> 0%
where the time goes in v1:
time: 278 us
  matrix products  133 us (48%)
  waiting for transfers between devices  71.5 us (26%)
  local copies, waits for them, and re-layouts  30.8 us (11%)
  starting transfers between devices  21.6 us (8%)
  other arithmetic  19.5 us (7%)
    dot_general x24, matrix products, one_block(): jnp.einsum('vqd,sd->vqs', query_block, store_flat, preferred_element_type...  133 us
    ppermute x5, waiting for transfers between devices, local(): lax.ppermute(everyone, ('group', 'shard'), [(d, d ^ reach) for d in range...  33.9 us
    all_to_all x1, waiting for transfers between devices, local(): lax.all_to_all(query_global, ('group', 'shard'), split_axis=1, concat_axi...  23.4 us
    gather x1, local copies, waits for them, and re-layouts, local(): storage = passage_slot[candidates].reshape(visit_count, PER_VISIT)  13.6 us
    ppermute x5, starting transfers between devices, local(): lax.ppermute(everyone, ('group', 'shard'), [(d, d ^ reach) for d in range...  8.84 us
    select_n x5, other arithmetic, local(): everyone = jnp.where(here & reach == 0, mine_first, theirs_first)  7.34 us
    all_to_all x1, waiting for transfers between devices, score_visits(): lax.all_to_all(visit_scores, ('group', 'shard'), split_axis=1, concat_axi...  7.18 us
    all_to_all x1, waiting for transfers between devices, local(): lax.all_to_all(send_local, ('group', 'shard'), split_axis=1, concat_axis=...  6.99 us
  transfers between devices with their start and end apart: 8, of which 7 were waited for; matrix products, arithmetic and copies ran while one was open for 7% of the time, Pallas kernels for 0%

profile of v1, /device:TPU:0, one launch (start us, length us, event | category | flops | bytes accessed | tf_op | source)
XLA Modules:
  0.0 277.5 jit_solution(18371286640700831930)
XLA Ops:
  9.6 5.6 %collective-permute-done.1 = bf16[32,32,128]{2,1,0:T(8,128)(2,1)S(1)} collective-permute-done((bf16[32,32,128]{2,1,0:T(8,128)(2,1)S(1)}, bf16[32,32,128]{2,1,0:T(8,128)(2,1)S(1)}, u32[]{:S(2)}, u32[]{:S(2)}) %collective-permute-start.1) | collective-permute-done | bytes 262176 | tf_op jit(solution)/shard_map/ppermute | solution.py:62
  18.0 21.8 %collective-permute-done.2 = bf16[64,32,128]{2,1,0:T(8,128)(2,1)S(1)} collective-permute-done((bf16[64,32,128]{2,1,0:T(8,128)(2,1)S(1)}, bf16[64,32,128]{2,1,0:T(8,128)(2,1)S(1)}, u32[]{:S(2)}, u32[]{:S(2)}) %collective-permute-start.2) | collective-permute-done | bytes 524320 | tf_op jit(solution)/shard_map/ppermute | solution.py:62
  46.2 13.6 %gather_fusion = s32[2560]{0:T(1024)S(1)} fusion(s32[2048]{0:T(1024)S(1)} %copy-done, s32[3072]{0:T(1024)S(1)} %pad_clamp_fusion), kind=kCustom, calls=%fused_computation | custom fusion | bytes 30720 | tf_op jit(solution)/shard_map/gather | solution.py:43
  69.4 23.4 %all-to-all-done.1 = s32[12,32,1]{0,2,1:T(1,128)S(1)} async-done(((s32[12,32,1]{0,2,1:T(1,128)}), s32[12,32,1]{0,2,1:T(1,128)S(1)}, u32[]{:S(2)}, u32[]{:S(2)}) %all-to-all-start.1) | async-done | bytes 1568 | tf_op jit(solution)/shard_map/all_to_all | solution.py:70
  98.4 7.0 %all-to-all-done = s32[32,1,240]{2,1,0:T(1,128)S(1)} async-done(((s32[32,1,240]{2,1,0:T(1,128)}), s32[32,1,240]{2,1,0:T(1,128)S(1)}, u32[]{:S(2)}, u32[]{:S(2)}) %all-to-all-start) | async-done | bytes 30752 | tf_op jit(solution)/shard_map/all_to_all | solution.py:73
  116.0 148.1 %while.11 = (s32[]{:T(128)}, f32[24,16,20]{2,1,0:T(8,128)S(1)}, s32[24,16,20]{2,1,0:T(8,128)S(1)}, bf16[24,16,32,128]{3,2,1,0:T(8,128)(2,1)}, bf16[4096,128]{1,0:T(8,128)(2,1)S(1)}, /*index=5*/s32[]{:T(128)}, f32[]{:T(128)}) while((s32[]{:T(128)}, f32[24,16,20]{2,1,0:T(8,128)S(1)}, s32[24,16,20]{2,1,0:T(8,128)S(1)}, ...), condition=%wide.region_7.8_spmd.clone, body=%wide.region_3.7_spmd.clone.sunk | while | flops 539029184 | bytes 1485401 | solution.py:31
  134.5 5.5 %convolution_reduce_fusion.2 = f32[16,32,64]{1,2,0:T(8,128)S(1)} fusion(bf16[64,64,128,1]{2,1,0,3:T(8,128)(2,1)S(1)} %bitcast.52, bf16[24,16,32,128]{3,2,1,0:T(8,128)(2,1)} %get-tuple-element.110, s32[]{:T(128)} %get-tuple-element.100), kind=kOutput, calls=%fused_computation.6.clone.1 | convolution fusion | flops 538935296 | bytes 1311232 | tf_op jit(solution)/shard_map/while/body/eval_jaxpr/vqd,sd->vqs/dot_general | solution.py:21
  140.6 5.5 %convolution_reduce_fusion.2 = f32[16,32,64]{1,2,0:T(8,128)S(1)} fusion(bf16[64,64,128,1]{2,1,0,3:T(8,128)(2,1)S(1)} %bitcast.52, bf16[24,16,32,128]{3,2,1,0:T(8,128)(2,1)} %get-tuple-element.110, s32[]{:T(128)} %get-tuple-element.100), kind=kOutput, calls=%fused_computation.6.clone.1 | convolution fusion | flops 538935296 | bytes 1311232 | tf_op jit(solution)/shard_map/while/body/eval_jaxpr/vqd,sd->vqs/dot_general | solution.py:21
  146.8 5.5 %convolution_reduce_fusion.2 = f32[16,32,64]{1,2,0:T(8,128)S(1)} fusion(bf16[64,64,128,1]{2,1,0,3:T(8,128)(2,1)S(1)} %bitcast.52, bf16[24,16,32,128]{3,2,1,0:T(8,128)(2,1)} %get-tuple-element.110, s32[]{:T(128)} %get-tuple-element.100), kind=kOutput, calls=%fused_computation.6.clone.1 | convolution fusion | flops 538935296 | bytes 1311232 | tf_op jit(solution)/shard_map/while/body/eval_jaxpr/vqd,sd->vqs/dot_general | solution.py:21
  153.0 5.5 %convolution_reduce_fusion.2 = f32[16,32,64]{1,2,0:T(8,128)S(1)} fusion(bf16[64,64,128,1]{2,1,0,3:T(8,128)(2,1)S(1)} %bitcast.52, bf16[24,16,32,128]{3,2,1,0:T(8,128)(2,1)} %get-tuple-element.110, s32[]{:T(128)} %get-tuple-element.100), kind=kOutput, calls=%fused_computation.6.clone.1 | convolution fusion | flops 538935296 | bytes 1311232 | tf_op jit(solution)/shard_map/while/body/eval_jaxpr/vqd,sd->vqs/dot_general | solution.py:21
  159.1 5.5 %convolution_reduce_fusion.2 = f32[16,32,64]{1,2,0:T(8,128)S(1)} fusion(bf16[64,64,128,1]{2,1,0,3:T(8,128)(2,1)S(1)} %bitcast.52, bf16[24,16,32,128]{3,2,1,0:T(8,128)(2,1)} %get-tuple-element.110, s32[]{:T(128)} %get-tuple-element.100), kind=kOutput, calls=%fused_computation.6.clone.1 | convolution fusion | flops 538935296 | bytes 1311232 | tf_op jit(solution)/shard_map/while/body/eval_jaxpr/vqd,sd->vqs/dot_general | solution.py:21
  171.5 5.5 %convolution_reduce_fusion.2 = f32[16,32,64]{1,2,0:T(8,128)S(1)} fusion(bf16[64,64,128,1]{2,1,0,3:T(8,128)(2,1)S(1)} %bitcast.52, bf16[24,16,32,128]{3,2,1,0:T(8,128)(2,1)} %get-tuple-element.110, s32[]{:T(128)} %get-tuple-element.100), kind=kOutput, calls=%fused_computation.6.clone.1 | convolution fusion | flops 538935296 | bytes 1311232 | tf_op jit(solution)/shard_map/while/body/eval_jaxpr/vqd,sd->vqs/dot_general | solution.py:21
  183.8 5.5 %convolution_reduce_fusion.2 = f32[16,32,64]{1,2,0:T(8,128)S(1)} fusion(bf16[64,64,128,1]{2,1,0,3:T(8,128)(2,1)S(1)} %bitcast.52, bf16[24,16,32,128]{3,2,1,0:T(8,128)(2,1)} %get-tuple-element.110, s32[]{:T(128)} %get-tuple-element.100), kind=kOutput, calls=%fused_computation.6.clone.1 | convolution fusion | flops 538935296 | bytes 1311232 | tf_op jit(solution)/shard_map/while/body/eval_jaxpr/vqd,sd->vqs/dot_general | solution.py:21
  190.0 5.5 %convolution_reduce_fusion.2 = f32[16,32,64]{1,2,0:T(8,128)S(1)} fusion(bf16[64,64,128,1]{2,1,0,3:T(8,128)(2,1)S(1)} %bitcast.52, bf16[24,16,32,128]{3,2,1,0:T(8,128)(2,1)} %get-tuple-element.110, s32[]{:T(128)} %get-tuple-element.100), kind=kOutput, calls=%fused_computation.6.clone.1 | convolution fusion | flops 538935296 | bytes 1311232 | tf_op jit(solution)/shard_map/while/body/eval_jaxpr/vqd,sd->vqs/dot_general | solution.py:21
  196.2 5.5 %convolution_reduce_fusion.2 = f32[16,32,64]{1,2,0:T(8,128)S(1)} fusion(bf16[64,64,128,1]{2,1,0,3:T(8,128)(2,1)S(1)} %bitcast.52, bf16[24,16,32,128]{3,2,1,0:T(8,128)(2,1)} %get-tuple-element.110, s32[]{:T(128)} %get-tuple-element.100), kind=kOutput, calls=%fused_computation.6.clone.1 | convolution fusion | flops 538935296 | bytes 1311232 | tf_op jit(solution)/shard_map/while/body/eval_jaxpr/vqd,sd->vqs/dot_general | solution.py:21
  202.4 5.5 %convolution_reduce_fusion.2 = f32[16,32,64]{1,2,0:T(8,128)S(1)} fusion(bf16[64,64,128,1]{2,1,0,3:T(8,128)(2,1)S(1)} %bitcast.52, bf16[24,16,32,128]{3,2,1,0:T(8,128)(2,1)} %get-tuple-element.110, s32[]{:T(128)} %get-tuple-element.100), kind=kOutput, calls=%fused_computation.6.clone.1 | convolution fusion | flops 538935296 | bytes 1311232 | tf_op jit(solution)/shard_map/while/body/eval_jaxpr/vqd,sd->vqs/dot_general | solution.py:21
  214.7 5.5 %convolution_reduce_fusion.2 = f32[16,32,64]{1,2,0:T(8,128)S(1)} fusion(bf16[64,64,128,1]{2,1,0,3:T(8,128)(2,1)S(1)} %bitcast.52, bf16[24,16,32,128]{3,2,1,0:T(8,128)(2,1)} %get-tuple-element.110, s32[]{:T(128)} %get-tuple-element.100), kind=kOutput, calls=%fused_computation.6.clone.1 | convolution fusion | flops 538935296 | bytes 1311232 | tf_op jit(solution)/shard_map/while/body/eval_jaxpr/vqd,sd->vqs/dot_general | solution.py:21
  220.9 5.5 %convolution_reduce_fusion.2 = f32[16,32,64]{1,2,0:T(8,128)S(1)} fusion(bf16[64,64,128,1]{2,1,0,3:T(8,128)(2,1)S(1)} %bitcast.52, bf16[24,16,32,128]{3,2,1,0:T(8,128)(2,1)} %get-tuple-element.110, s32[]{:T(128)} %get-tuple-element.100), kind=kOutput, calls=%fused_computation.6.clone.1 | convolution fusion | flops 538935296 | bytes 1311232 | tf_op jit(solution)/shard_map/while/body/eval_jaxpr/vqd,sd->vqs/dot_general | solution.py:21
  227.0 5.5 %convolution_reduce_fusion.2 = f32[16,32,64]{1,2,0:T(8,128)S(1)} fusion(bf16[64,64,128,1]{2,1,0,3:T(8,128)(2,1)S(1)} %bitcast.52, bf16[24,16,32,128]{3,2,1,0:T(8,128)(2,1)} %get-tuple-element.110, s32[]{:T(128)} %get-tuple-element.100), kind=kOutput, calls=%fused_computation.6.clone.1 | convolution fusion | flops 538935296 | bytes 1311232 | tf_op jit(solution)/shard_map/while/body/eval_jaxpr/vqd,sd->vqs/dot_general | solution.py:21
  233.2 5.5 %convolution_reduce_fusion.2 = f32[16,32,64]{1,2,0:T(8,128)S(1)} fusion(bf16[64,64,128,1]{2,1,0,3:T(8,128)(2,1)S(1)} %bitcast.52, bf16[24,16,32,128]{3,2,1,0:T(8,128)(2,1)} %get-tuple-element.110, s32[]{:T(128)} %get-tuple-element.100), kind=kOutput, calls=%fused_computation.6.clone.1 | convolution fusion | flops 538935296 | bytes 1311232 | tf_op jit(solution)/shard_map/while/body/eval_jaxpr/vqd,sd->vqs/dot_general | solution.py:21
  239.4 5.5 %convolution_reduce_fusion.2 = f32[16,32,64]{1,2,0:T(8,128)S(1)} fusion(bf16[64,64,128,1]{2,1,0,3:T(8,128)(2,1)S(1)} %bitcast.52, bf16[24,16,32,128]{3,2,1,0:T(8,128)(2,1)} %get-tuple-element.110, s32[]{:T(128)} %get-tuple-element.100), kind=kOutput, calls=%fused_computation.6.clone.1 | convolution fusion | flops 538935296 | bytes 1311232 | tf_op jit(solution)/shard_map/while/body/eval_jaxpr/vqd,sd->vqs/dot_general | solution.py:21
  245.6 5.5 %convolution_reduce_fusion.2 = f32[16,32,64]{1,2,0:T(8,128)S(1)} fusion(bf16[64,64,128,1]{2,1,0,3:T(8,128)(2,1)S(1)} %bitcast.52, bf16[24,16,32,128]{3,2,1,0:T(8,128)(2,1)} %get-tuple-element.110, s32[]{:T(128)} %get-tuple-element.100), kind=kOutput, calls=%fused_computation.6.clone.1 | convolution fusion | flops 538935296 | bytes 1311232 | tf_op jit(solution)/shard_map/while/body/eval_jaxpr/vqd,sd->vqs/dot_general | solution.py:21
  257.9 5.5 %convolution_reduce_fusion.2 = f32[16,32,64]{1,2,0:T(8,128)S(1)} fusion(bf16[64,64,128,1]{2,1,0,3:T(8,128)(2,1)S(1)} %bitcast.52, bf16[24,16,32,128]{3,2,1,0:T(8,128)(2,1)} %get-tuple-element.110, s32[]{:T(128)} %get-tuple-element.100), kind=kOutput, calls=%fused_computation.6.clone.1 | convolution fusion | flops 538935296 | bytes 1311232 | tf_op jit(solution)/shard_map/while/body/eval_jaxpr/vqd,sd->vqs/dot_general | solution.py:21
  267.6 7.2 %all-to-all-done.2 = f32[32,1,240]{2,1,0:T(1,128)S(1)} async-done(((f32[32,1,240]{2,1,0:T(1,128)}), f32[32,1,240]{2,1,0:T(1,128)S(1)}, u32[]{:S(2)}, u32[]{:S(2)}) %all-to-all-start.2) | async-done | bytes 30752 | tf_op jit(solution)/shard_map/all_to_all | solution.py:33
  (237 shorter events, 103.6 us)
Async XLA Ops:
  0.0 46.1 %copy-start = (s32[2048]{0:T(1024)S(1)}, s32[2048]{0:T(1024)}, u32[]{:S(2)}) copy-start(s32[2048]{0:T(1024)} %param.9) | copy-start | bytes 24580
  0.0 6.7 %collective-permute-start = (bf16[16,32,128]{2,1,0:T(8,128)(2,1)}, bf16[16,32,128]{2,1,0:T(8,128)(2,1)S(1)}, u32[]{:S(2)}, u32[]{:S(2)}) collective-permute-start(bf16[16,32,128]{2,1,0:T(8,128)(2,1)} %param.6), channel_id=1, source_target_pairs={{0,1},{1,0},{2,3},{3,2},{4,5},{5,4},{6,7},{7,6},{8,9},{9,8},{10,11... | collective-permute-start | bytes 393224 | tf_op jit(solution)/shard_map/ppermute | solution.py:62
  7.7 7.5 %collective-permute-start.1 = (bf16[32,32,128]{2,1,0:T(8,128)(2,1)S(1)}, bf16[32,32,128]{2,1,0:T(8,128)(2,1)S(1)}, u32[]{:S(2)}, u32[]{:S(2)}) collective-permute-start(bf16[32,32,128]{2,1,0:T(8,128)(2,1)S(1)} %maximum_select_fusion.4), channel_id=1, source_target_pairs={{0,2},{1,3},{2,0},{3,1},{4,6},{5,7},{6,4},{7,5},{8,10},{9,11},{10,... | collective-permute-start | bytes 786440 | tf_op jit(solution)/shard_map/ppermute | solution.py:62
  15.3 24.4 %collective-permute-start.2 = (bf16[64,32,128]{2,1,0:T(8,128)(2,1)S(1)}, bf16[64,32,128]{2,1,0:T(8,128)(2,1)S(1)}, u32[]{:S(2)}, u32[]{:S(2)}) collective-permute-start(bf16[64,32,128]{2,1,0:T(8,128)(2,1)S(1)} %maximum_select_fusion.3), channel_id=1, source_target_pairs={{0,4},{1,5},{2,6},{3,7},{4,0},{5,1},{6,2},{7,3},{8,12},{9,13},{10,... | collective-permute-start | bytes 1572872 | tf_op jit(solution)/shard_map/ppermute | solution.py:62
  18.0 28.1 %copy-start.1 = (s32[16,160]{1,0:T(8,128)S(1)}, s32[16,160]{1,0:T(8,128)}, u32[]{:S(2)}) copy-start(s32[16,160]{1,0:T(8,128)} %param.8) | copy-start | bytes 30724
  39.9 2.9 %collective-permute-start.3 = (bf16[128,32,128]{2,1,0:T(8,128)(2,1)S(1)}, bf16[128,32,128]{2,1,0:T(8,128)(2,1)}, u32[]{:S(2)}, u32[]{:S(2)}) collective-permute-start(bf16[128,32,128]{2,1,0:T(8,128)(2,1)S(1)} %maximum_select_fusion.2), channel_id=1, source_target_pairs={{0,8},{1,9},{2,10},{3,11},{4,12},{5,13},{6,14},{7,15},{8,0},{9,1},... | collective-permute-start | bytes 3145736 | tf_op jit(solution)/shard_map/ppermute | solution.py:62
  44.8 62.1 %collective-permute-start.4 = (bf16[256,32,128]{2,1,0:T(8,128)(2,1)S(1)}, bf16[256,32,128]{2,1,0:T(8,128)(2,1)}, u32[]{:S(2)}, u32[]{:S(2)}) collective-permute-start(bf16[256,32,128]{2,1,0:T(8,128)(2,1)S(1)} %maximum_select_fusion.1), channel_id=1, source_target_pairs={{0,16},{1,17},{2,18},{3,19},{4,20},{5,21},{6,22},{7,23},{8,24},{9,... | collective-permute-start | bytes 6291464 | tf_op jit(solution)/shard_map/ppermute | solution.py:62
  62.5 30.3 %all-to-all-start.1 = ((s32[12,32,1]{0,2,1:T(1,128)}), s32[12,32,1]{0,2,1:T(1,128)S(1)}, u32[]{:S(2)}, u32[]{:S(2)}) async-start(s32[12,32,1]{0,2,1:T(1,128)} %copy.19), calls=%async_computation.1 | async-start | bytes 32768 | tf_op jit(solution)/shard_map/all_to_all | solution.py:70
  92.8 12.6 %all-to-all-start = ((s32[32,1,240]{2,1,0:T(1,128)}), s32[32,1,240]{2,1,0:T(1,128)S(1)}, u32[]{:S(2)}, u32[]{:S(2)}) async-start(s32[32,1,240]{2,1,0:T(1,128)} %reshape.105), calls=%async_computation | async-start | bytes 65536 | tf_op jit(solution)/shard_map/all_to_all | solution.py:73
  111.0 5.0 %copy-start.2 = (bf16[64,64,128]{2,1,0:T(8,128)(2,1)S(1)}, bf16[64,64,128]{2,1,0:T(8,128)(2,1)}, u32[]{:S(2)}) copy-start(bf16[64,64,128]{2,1,0:T(8,128)(2,1)} %param.7) | copy-start | bytes 3145732
  265.0 9.8 %all-to-all-start.2 = ((f32[32,1,240]{2,1,0:T(1,128)}), f32[32,1,240]{2,1,0:T(1,128)S(1)}, u32[]{:S(2)}, u32[]{:S(2)}) async-start(f32[32,1,240]{2,1,0:T(1,128)} %reshape.107), calls=%async_computation.2 | async-start | bytes 65536 | tf_op jit(solution)/shard_map/all_to_all | solution.py:33
